TPU v7x, 128 devices: a whole 4x4x4 slice. The times are simulated.
128 devices in a mesh: tm: 16 (over y, x), head: 8 (over z, core).
Axes of the slice: x: 4, y: 4, z: 4, core: 2. Of those that a mesh axis runs over, the one named last changes fastest.
Arguments:
- inputs: bfloat16 [8192, 2048], P('tm', 'head'), may hold values from -6 to 6
- in_weight: bfloat16 [2048, 2048], P(None, 'head'), may hold values from -0.00036621094 to 0.00036621094
- rec_weight: float32 [16, 128, 128], P('head'), may hold values from -1 to 1, as said below
- bias: float32 [2048], P('head'), may hold values from -0.0012207031 to 0.0012207031
- initial: float32 [2048], P('head'), may hold values from -0.25 to 0.25
- guess: float32 [8192, 2048], P('tm', 'head'), may hold values from -0.25 to 0.25
Outputs:
- trajectory: float32 [8192, 2048], P('tm', 'head')
- next_guess: float32 [8192, 2048], P('tm', 'head')
Inputs may be any that keep to these rules, and one draw needn't show every extreme that they name: `rec_weight`: each head's matrix has operator norm below one.
All inputs are finite; a program needn't handle non-finite values.
Results may differ from a plain program's by a relative error of at most 0.0003.
Values may be sent and summed in bfloat16 or wider, within the bound.
A program may use at most 128 MiB of HBM per device.

v0:
```python
import jax
import jax.numpy as jnp
from jax import lax
from jax.sharding import Mesh
from jax.sharding import PartitionSpec as P

BLOCK = 16
SWEEPS = 2
TM = ("tm_0", "tm_1")


def passed_along(value, axis, by):
    count = lax.axis_size(axis)
    pairs = [(i, i + by) for i in range(count) if 0 <= i + by < count]
    return lax.ppermute(value, axis, pairs)


def neutral_like(value, identity):
    return jax.tree.map(
        lambda a, e: jnp.broadcast_to(jnp.asarray(e, a.dtype), a.shape), value, identity
    )


def prefix_by_axis(value, axes, combine, identity):
    before = start = neutral_like(value, identity)
    running = value
    for axis in reversed(axes):
        count, here = (lax.axis_size(axis), lax.axis_index(axis))
        pieces = jax.tree.map(lambda part: lax.all_gather(part, axis), running)
        inside, running = (start, start)
        for k in range(count):
            passed = k < here
            running = combine(running, jax.tree.map(lambda part: part[k], pieces))
            inside = jax.tree.map(lambda new, old: jnp.where(passed, new, old), running, inside)
        before = combine(inside, before)
    return before


def chain_maps(earlier, later):
    matrix = jnp.einsum("nhij,nhjk->nhik", later[0], earlier[0], precision=lax.Precision.HIGHEST)
    vector = (
        jnp.einsum("nhij,nhj->nhi", later[0], earlier[1], precision=lax.Precision.HIGHEST)
        + later[1]
    )
    return (matrix, vector)


def chain_slab(earlier, later):
    matrix = jnp.einsum("hij,hjk->hik", later[0], earlier[0], precision=lax.Precision.HIGHEST)
    vector = (
        jnp.einsum("hij,hj->hi", later[0], earlier[1], precision=lax.Precision.HIGHEST) + later[1]
    )
    return (matrix, vector)


def shards(inputs, in_weight, rec_weight, bias, initial, guess):
    slab_len, width = guess.shape
    local_heads, head_units = (rec_weight.shape[0], rec_weight.shape[1])
    blocks = slab_len // BLOCK
    drive = (
        jnp.dot(
            lax.all_gather(inputs, "head", axis=1, tiled=True),
            in_weight,
            preferred_element_type=jnp.float32,
        )
        + bias
    )
    drive_grid = drive.reshape(blocks, BLOCK, local_heads, head_units)
    is_first = lax.axis_index(TM) == 0
    start_state = initial.reshape(local_heads, head_units)
    identity = jnp.broadcast_to(
        jnp.eye(head_units, dtype=jnp.float32), (local_heads, head_units, head_units)
    )
    current = guess
    for repeat in range(SWEEPS):
        before = passed_along(current[-1], TM, 1)
        before = jnp.where(is_first, initial, before)
        current_grid = current.reshape(blocks, BLOCK, local_heads, head_units)
        block_first = jnp.concatenate(
            [before.reshape(1, local_heads, head_units), current_grid[:-1, BLOCK - 1]], axis=0
        )

        def compose(step, carry):
            matrix, vector, slope_grid, offset_grid = carry
            previous = lax.dynamic_index_in_dim(
                current_grid, jnp.maximum(step - 1, 0), 1, keepdims=False
            )
            prior_now = jnp.where(step == 0, block_first, previous)
            drive_now = lax.dynamic_index_in_dim(drive_grid, step, 1, keepdims=False)
            linear = jnp.einsum(
                "hij,nhj->nhi", rec_weight, prior_now, precision=lax.Precision.HIGHEST
            )
            value = jnp.tanh(linear + drive_now)
            slope_now = 1.0 - value * value
            offset_now = value - slope_now * linear
            matrix = slope_now[..., None] * jnp.einsum(
                "hij,nhjk->nhik", rec_weight, matrix, precision=lax.Precision.HIGHEST
            )
            vector = (
                slope_now
                * jnp.einsum("hij,nhj->nhi", rec_weight, vector, precision=lax.Precision.HIGHEST)
                + offset_now
            )
            slope_grid = lax.dynamic_update_index_in_dim(slope_grid, slope_now, step, 1)
            offset_grid = lax.dynamic_update_index_in_dim(offset_grid, offset_now, step, 1)
            return (matrix, vector, slope_grid, offset_grid)

        zero_grid = jnp.zeros((blocks, BLOCK, local_heads, head_units), jnp.float32)
        start_maps = (
            jnp.broadcast_to(identity[None], (blocks, local_heads, head_units, head_units)),
            jnp.zeros((blocks, local_heads, head_units), jnp.float32),
            zero_grid,
            zero_grid,
        )
        block_matrix, block_vector, slope_grid, offset_grid = lax.fori_loop(
            0, BLOCK, compose, start_maps
        )
        prefix_matrix, prefix_vector = lax.associative_scan(
            chain_maps, (block_matrix, block_vector)
        )
        slab_matrix, slab_vector = (prefix_matrix[-1], prefix_vector[-1])
        zero_vector = jnp.zeros((local_heads, head_units), jnp.float32)
        earlier_matrix, earlier_vector = prefix_by_axis(
            (slab_matrix, slab_vector), TM, chain_slab, (identity, zero_vector)
        )
        entering = (
            jnp.einsum("hij,hj->hi", earlier_matrix, start_state, precision=lax.Precision.HIGHEST)
            + earlier_vector
        )
        inner = (
            jnp.einsum(
                "nhij,hj->nhi", prefix_matrix[:-1], entering, precision=lax.Precision.HIGHEST
            )
            + prefix_vector[:-1]
        )
        block_start = jnp.concatenate([entering[None], inner], axis=0)

        def advance(step, carry):
            state, state_grid = carry
            slope_now = lax.dynamic_index_in_dim(slope_grid, step, 1, keepdims=False)
            offset_now = lax.dynamic_index_in_dim(offset_grid, step, 1, keepdims=False)
            state = (
                slope_now
                * jnp.einsum("hij,nhj->nhi", rec_weight, state, precision=lax.Precision.HIGHEST)
                + offset_now
            )
            state_grid = lax.dynamic_update_index_in_dim(state_grid, state, step, 1)
            return (state, state_grid)

        ending, state_grid = lax.fori_loop(0, BLOCK, advance, (block_start, zero_grid))
        current = state_grid.reshape(slab_len, width)
    ahead = passed_along(current, TM, -1)
    is_last = lax.axis_index(TM) == lax.axis_size(TM) - 1
    tail = jnp.broadcast_to(current[-1][None, :], (slab_len, width))
    next_guess = jnp.where(is_last, tail, ahead)
    return (current, next_guess)


def solution(mesh):
    finer = Mesh(mesh.devices.reshape(4, 4, mesh.shape["head"]), ("tm_0", "tm_1", "head"))
    in_specs = (
        P(TM, "head"),
        P(None, "head"),
        P("head", None, None),
        P("head"),
        P("head"),
        P(TM, "head"),
    )
    out_specs = (P(TM, "head"), P(TM, "head"))
    return jax.shard_map(
        shards, mesh=finer, in_specs=in_specs, out_specs=out_specs, check_vma=False
    )
```

profile of v0, /device:TPU:6, one launch (start us, length us, event | category | flops | bytes accessed | tf_op | source)
XLA Modules:
  0.0 808.5 jit_solution(7641998961345186644)
XLA Ops:
  14.1 24.9 %all-gather.8.cloned.1.call-done = bf16[512,2048]{1,0:T(8,128)(2,1)} async-done(((bf16[512,256]{1,0:T(8,128)(2,1)}), bf16[512,2048]{1,0:T(8,128)(2,1)}) %all-gather.8.cloned.1.call-update) | async-done | bytes 2097168 | tf_op jit(solution)/shard_map/all_gather | solution.py:62
  44.6 127.1 %while.76 = (s32[]{:T(128)}, f32[32,2,128,128]{2,3,0,1:T(8,128)}, f32[32,2,128]{2,0,1:T(8,128)S(1)}, f32[32,16,2,128]{3,0,2,1:T(8,128)S(1)}, f32[32,16,2,128]{3,...) while((s32[]{:T(128)}, f32[32,2,128,128]{2,3,0,1:T(8,128)}, ...), condition=%wide.region_1.2_spmd.clone, body=%wide.region_0.1_spmd.clone.sunk | while | flops 1636925440 | bytes 17760424 | solution.py:115
  249.6 7.0 pad.131
  257.8 10.2 %pad.130 = f32[16,2,128,128]{3,2,1,0:T(8,128)} pad(f32[8,2,128,128]{3,2,1,0:T(8,128)} %pad_maximum_fusion.2, f32[]{:T(128)} %constant.182.clone.1), padding=0_1_1x0_0_0x0_0_0x0_0_0 | pad | bytes 3145732 | tf_op jit(solution)/shard_map/pad | solution.py:118
  274.2 12.2 %pad.132 = f32[32,2,128,128]{3,2,1,0:T(8,128)} pad(f32[16,2,128,128]{3,2,1,0:T(8,128)S(1)} %pad_maximum_fusion, f32[]{:T(128)} %constant.182.clone.1), padding=0_1_1x0_0_0x0_0_0x0_0_0 | pad | bytes 6291460 | tf_op jit(solution)/shard_map/pad | solution.py:118
  286.4 18.6 %pad.133 = f32[32,2,128,128]{3,2,1,0:T(8,128)} pad(f32[16,2,128,128]{3,2,1,0:T(8,128)} %add.459, f32[]{:T(128)} %constant.182.clone.1), padding=1_0_1x0_0_0x0_0_0x0_0_0 | pad | bytes 6291460 | tf_op jit(solution)/shard_map/pad | solution.py:118
  306.2 13.5 %all_gather.40 = f32[4,2,128,128]{3,2,1,0:T(8,128)S(1)} all-gather(f32[1,2,128,128]{3,2,1,0:T(8,128)S(1)} %slice_add_fusion.1), channel_id=1, replica_groups=mesh['tm_0'=4,'tm_1'=4,'head'=8] {'tm_1'}, dimensions={0}, use_global_device_ids=true | all-gather | bytes 655360 | tf_op jit(solution)/shard_map/all_gather | solution.py:29
  323.1 13.1 %all-gather = f32[8,128,128]{2,1,0:T(8,128)S(1)} all-gather(f32[2,128,128]{2,1,0:T(8,128)S(1)} %fusion.133), channel_id=2, replica_groups=mesh['tm_0'=4,'tm_1'=4,'head'=8] {'tm_0'}, dimensions={0}, use_global_device_ids=true | all-gather | bytes 655360 | tf_op jit(solution)/shard_map/all_gather | solution.py:29
  362.6 9.4 %all-gather.4 = f32[4,2,128]{2,1,0:T(2,128)S(1)} all-gather(f32[1,2,128]{2,1,0:T(2,128)S(1)} %get-tuple-element.885), channel_id=3, replica_groups=mesh['tm_0'=4,'tm_1'=4,'head'=8] {'tm_0'}, dimensions={0}, use_global_device_ids=true | all-gather | bytes 5120 | tf_op jit(solution)/shard_map/all_gather | solution.py:29
  375.2 12.1 %pad.208 = f32[31,2,128,128]{3,2,1,0:T(8,128)} pad(f32[16,2,128,128]{3,2,1,0:T(8,128)S(1)} %pad_maximum_fusion, f32[]{:T(128)} %constant.182.clone.1), padding=0_0_1x0_0_0x0_0_0x0_0_0 | pad | bytes 6160388 | tf_op jit(solution)/shard_map/slice | solution.py:132
  394.8 17.8 %while.74 = (s32[]{:T(128)}, f32[32,2,128]{2,0,1:T(8,128)S(1)}, f32[32,16,2,128]{3,0,2,1:T(8,128)S(1)}, f32[32,16,2,128]{3,0,2,1:T(8,128)}, f32[2,128,128]{2,1,0...) while((s32[]{:T(128)}, f32[32,2,128]{2,0,1:T(8,128)S(1)}, f32[32,16,2,128]{3,0,2,1:T(8,128)S(1)}, ...), condition=%wide.region_3.4_spmd, body=%wide.region_2.3_spmd.sunk | while | flops 12599298 | bytes 360529 | solution.py:150
  421.3 151.0 %while.77 = (s32[]{:T(128)}, f32[32,2,128,128]{2,3,0,1:T(8,128)}, f32[32,2,128]{2,0,1:T(8,128)S(1)}, f32[32,16,2,128]{3,0,2,1:T(8,128)S(1)}, f32[32,16,2,128]{3,...) while((s32[]{:T(128)}, f32[32,2,128,128]{2,3,0,1:T(8,128)}, ...), condition=%wide.region_5.6_spmd.clone, body=%wide.region_4.5_spmd.clone.sunk | while | flops 1636925440 | bytes 17694888 | solution.py:115
  629.9 7.0 pad.151
  638.1 10.2 %pad.150 = f32[16,2,128,128]{3,2,1,0:T(8,128)} pad(f32[8,2,128,128]{3,2,1,0:T(8,128)} %pad_maximum_fusion.3, f32[]{:T(128)} %constant.182.clone.1), padding=0_1_1x0_0_0x0_0_0x0_0_0 | pad | bytes 3145732 | tf_op jit(solution)/shard_map/pad | solution.py:118
  654.5 12.2 %pad.152 = f32[32,2,128,128]{3,2,1,0:T(8,128)} pad(f32[16,2,128,128]{3,2,1,0:T(8,128)S(1)} %pad_maximum_fusion.1, f32[]{:T(128)} %constant.182.clone.1), padding=0_1_1x0_0_0x0_0_0x0_0_0 | pad | bytes 6291460 | tf_op jit(solution)/shard_map/pad | solution.py:118
  666.7 18.6 %pad.153 = f32[32,2,128,128]{3,2,1,0:T(8,128)} pad(f32[16,2,128,128]{3,2,1,0:T(8,128)} %add.489, f32[]{:T(128)} %constant.182.clone.1), padding=1_0_1x0_0_0x0_0_0x0_0_0 | pad | bytes 6291460 | tf_op jit(solution)/shard_map/pad | solution.py:118
  686.3 12.9 %all_gather.46 = f32[4,2,128,128]{3,2,1,0:T(8,128)S(1)} all-gather(f32[1,2,128,128]{3,2,1,0:T(8,128)S(1)} %slice_add_fusion), channel_id=1, replica_groups=mesh['tm_0'=4,'tm_1'=4,'head'=8] {'tm_1'}, dimensions={0}, use_global_device_ids=true | all-gather | bytes 655360 | tf_op jit(solution)/shard_map/all_gather | solution.py:29
  701.2 12.8 %all-gather.2 = f32[8,128,128]{2,1,0:T(8,128)S(1)} all-gather(f32[2,128,128]{2,1,0:T(8,128)S(1)} %fusion.143), channel_id=4, replica_groups=mesh['tm_0'=4,'tm_1'=4,'head'=8] {'tm_0'}, dimensions={0}, use_global_device_ids=true | all-gather | bytes 655360 | tf_op jit(solution)/shard_map/all_gather | solution.py:29
  725.5 8.6 %all_gather.49 = f32[4,2,128]{2,1,0:T(2,128)S(1)} all-gather(f32[1,2,128]{2,1,0:T(2,128)S(1)} %slice_add_fusion.22), channel_id=1, replica_groups=mesh['tm_0'=4,'tm_1'=4,'head'=8] {'tm_1'}, dimensions={0}, use_global_device_ids=true | all-gather | bytes 5120 | tf_op jit(solution)/shard_map/all_gather | solution.py:29
  736.0 8.8 %all-gather.5 = f32[4,2,128]{2,1,0:T(2,128)S(1)} all-gather(f32[1,2,128]{2,1,0:T(2,128)S(1)} %get-tuple-element.883), channel_id=5, replica_groups=mesh['tm_0'=4,'tm_1'=4,'head'=8] {'tm_0'}, dimensions={0}, use_global_device_ids=true | all-gather | bytes 5120 | tf_op jit(solution)/shard_map/all_gather | solution.py:29
  749.1 12.1 %pad.212 = f32[31,2,128,128]{3,2,1,0:T(8,128)} pad(f32[16,2,128,128]{3,2,1,0:T(8,128)S(1)} %pad_maximum_fusion.1, f32[]{:T(128)} %constant.182.clone.1), padding=0_0_1x0_0_0x0_0_0x0_0_0 | pad | bytes 6160388 | tf_op jit(solution)/shard_map/slice | solution.py:132
  761.4 6.9 fusion.26
  768.4 18.9 %while.75 = (s32[]{:T(128)}, f32[32,2,128]{2,0,1:T(8,128)S(1)}, f32[32,16,2,128]{3,2,1,0:T(2,128)S(1)}, f32[32,16,2,128]{3,0,2,1:T(8,128)}, f32[2,128,128]{2,1,0...) while((s32[]{:T(128)}, f32[32,2,128]{2,0,1:T(8,128)S(1)}, f32[32,16,2,128]{3,2,1,0:T(2,128)S(1)}, ...), condition=%wide.region_7.8_spmd, body=%wide.region_6.7_spmd.sunk | while | flops 12599298 | bytes 393301 | solution.py:150
  789.3 11.2 %collective-permute-done.2 = f32[512,256]{1,0:T(8,128)S(1)} collective-permute-done((f32[512,256]{1,0:T(8,128)S(1)}, f32[512,256]{1,0:T(8,128)S(1)}, u32[]{:S(2)}, u32[]{:S(2)}) %collective-permute-start.2) | collective-permute-done | bytes 524320 | tf_op jit(solution)/shard_map/ppermute | solution.py:15
  (643 shorter events, 548.3 us)
Async XLA Ops:
  7.2 31.8 %copy-start = (bf16[2048,256]{1,0:T(8,128)(2,1)S(1)}, bf16[2048,256]{1,0:T(8,128)(2,1)}, u32[]{:S(2)}) copy-start(bf16[2048,256]{1,0:T(8,128)(2,1)} %param.15) | copy-start | bytes 3145732
  7.2 31.8 %all-gather.8.cloned.1.call-start = ((), (), s32[]{:S(2)}) async-start(), calls=%async_computation | async-start | bytes 2359296 | tf_op jit(solution)/shard_map/all_gather | solution.py:62
  8.6 5.5 collective-permute-start
  13.5 28.4 %copy-start.29 = (f32[128,128]{0,1:T(8,128)}, f32[128,128]{0,1:T(8,128)S(1)}, u32[]{:S(2)}) copy-start(f32[128,128]{0,1:T(8,128)S(1)} %copy.49) | copy-start | bytes 196612
  171.7 40.9 %copy-start.35 = (f32[32,2,128]{2,1,0:T(2,128)}, f32[32,2,128]{2,1,0:T(2,128)S(1)}, u32[]{:S(2)}) copy-start(f32[32,2,128]{2,1,0:T(2,128)S(1)} %copy.57) | copy-start | bytes 98308
  182.8 66.8 %copy-start.7 = (f32[16,2,128,128]{3,2,1,0:T(8,128)}, f32[16,2,128,128]{3,2,1,0:T(8,128)S(1)}, u32[]{:S(2)}) copy-start(f32[16,2,128,128]{3,2,1,0:T(8,128)S(1)} %fusion.32) | copy-start | bytes 6291460
  193.5 29.5 %slice-start.5 = ((f32[4,2,128,128]{3,2,1,0:T(8,128)}), f32[1,2,128,128]{3,2,1,0:T(8,128)S(1)}, s32[]{:S(2)}) async-start(f32[4,2,128,128]{3,2,1,0:T(8,128)} %copy-done.14), calls=%async_computation.6 | async-start | bytes 262144 | tf_op jit(solution)/shard_map/slice | solution.py:118
  305.0 33.0 %copy-start.6 = (f32[32,2,128,128]{3,2,1,0:T(8,128)S(1)}, f32[32,2,128,128]{3,2,1,0:T(8,128)}, u32[]{:S(2)}) copy-start(f32[32,2,128,128]{3,2,1,0:T(8,128)} %copy.53) | copy-start | bytes 12582916
  320.0 18.0 %copy-start.39 = (f32[2,128,1]{1,0,2:T(2,128)}, f32[2,128,1]{1,0,2:T(2,128)S(1)}, u32[]{:S(2)}) copy-start(f32[2,128,1]{1,0,2:T(2,128)S(1)} %broadcast.125) | copy-start | bytes 3076
  321.2 20.0 %copy-start.36 = (f32[32,2,128]{2,1,0:T(2,128)S(1)}, f32[32,2,128]{2,1,0:T(2,128)}, u32[]{:S(2)}) copy-start(f32[32,2,128]{2,1,0:T(2,128)} %copy-done.35) | copy-start | bytes 98308
  321.2 20.0 %slice-start.6 = ((f32[32,2,128]{2,1,0:T(2,128)}), f32[1,2,128]{2,1,0:T(2,128)S(1)}, s32[]{:S(2)}) async-start(f32[32,2,128]{2,1,0:T(2,128)} %copy-done.35), calls=%async_computation.7 | async-start | bytes 2048 | tf_op jit(solution)/shard_map/slice | solution.py:118
  352.0 21.7 %copy-start.24 = (f32[2,128,128]{2,1,0:T(8,128)S(1)}, f32[2,128,128]{2,1,0:T(8,128)}, u32[]{:S(2)}) copy-start(f32[2,128,128]{2,1,0:T(8,128)} %fusion.158) | copy-start | bytes 393220
  394.8 23.8 %copy-start.30 = (f32[128,128]{0,1:T(8,128)S(1)}, f32[128,128]{0,1:T(8,128)}, u32[]{:S(2)}) copy-start(f32[128,128]{0,1:T(8,128)} %copy-done.29) | copy-start | bytes 196612
  413.1 5.5 collective-permute-start.1
  583.4 46.5 %copy-start.8 = (f32[16,2,128,128]{3,2,1,0:T(8,128)}, f32[16,2,128,128]{3,2,1,0:T(8,128)S(1)}, u32[]{:S(2)}) copy-start(f32[16,2,128,128]{3,2,1,0:T(8,128)S(1)} %fusion.30) | copy-start | bytes 6291460
  666.7 32.5 %copy-start.40 = (f32[2,128,1]{1,0,2:T(2,128)S(1)}, f32[2,128,1]{1,0,2:T(2,128)}, u32[]{:S(2)}) copy-start(f32[2,128,1]{1,0,2:T(2,128)} %copy-done.39) | copy-start | bytes 3076
  686.3 29.8 %copy-start.4 = (f32[32,2,128,128]{3,2,1,0:T(8,128)S(1)}, f32[32,2,128,128]{3,2,1,0:T(8,128)}, u32[]{:S(2)}) copy-start(f32[32,2,128,128]{3,2,1,0:T(8,128)} %copy.63) | copy-start | bytes 12582916
  699.2 16.9 %copy-start.37 = (f32[15,2,128]{2,1,0:T(2,128)S(1)}, f32[15,2,128]{2,1,0:T(2,128)}, u32[]{:S(2)}) copy-start(f32[15,2,128]{2,1,0:T(2,128)} %slice_add_fusion.4) | copy-start | bytes 46084
  701.2 18.0 %copy-start.43 = (f32[1,2,128]{2,1,0:T(2,128)S(1)}, f32[1,2,128]{2,1,0:T(2,128)}, u32[]{:S(2)}) copy-start(f32[1,2,128]{2,1,0:T(2,128)} %slice.641) | copy-start | bytes 3076
  724.5 24.2 %copy-start.42 = (f32[256]{0:T(256)S(1)}, f32[256]{0:T(256)}, u32[]{:S(2)}) copy-start(f32[256]{0:T(256)} %param.18) | copy-start | bytes 3076
  724.7 23.1 %copy-start.23 = (f32[2,128,128]{2,1,0:T(8,128)S(1)}, f32[2,128,128]{2,1,0:T(8,128)}, u32[]{:S(2)}) copy-start(f32[2,128,128]{2,1,0:T(8,128)} %fusion.150) | copy-start | bytes 393220
  768.4 33.0 %copy-start.1 = (bf16[2048,256]{1,0:T(8,128)(2,1)S(1)}, bf16[2048,256]{1,0:T(8,128)(2,1)}, u32[]{:S(2)}) copy-start(bf16[2048,256]{1,0:T(8,128)(2,1)} %param.15) | copy-start | bytes 3145732
  787.3 14.0 %copy-start.31 = (f32[64,8,2,128]{3,1,2,0:T(8,128)}, f32[64,8,2,128]{3,1,2,0:T(8,128)S(1)}, u32[]{:S(2)}) copy-start(f32[64,8,2,128]{3,1,2,0:T(8,128)S(1)} %copy.220) | copy-start | bytes 1572868
  787.4 13.2 %collective-permute-start.2 = (f32[512,256]{1,0:T(8,128)S(1)}, f32[512,256]{1,0:T(8,128)S(1)}, u32[]{:S(2)}, u32[]{:S(2)}) collective-permute-start(f32[512,256]{1,0:T(8,128)S(1)} %bitcast.627), channel_id=1, source_target_pairs={{8,0},{16,8},{24,16},{32,24},{40,32},{48,40},{56,48},{64,56},{72,6... | collective-permute-start | bytes 1572872 | tf_op jit(solution)/shard_map/ppermute | solution.py:15
  (31 other events, 129.0 us)
Sparse Core Ops, SparseCore 0:
  9.7 29.2 all-gather.7
where the time goes:
time: 823 us; the launch traced here: 808 us
  matrix products  335 us (41%)
  local copies, waits for them, and re-layouts  284 us (35%)
  blocking collectives  85.8 us (10%)
  waiting for transfers between devices  39.3 us (5%)
  other arithmetic  38.2 us (5%)
  between operations  15.5 us (2%)
  starting transfers between devices  8.84 us (1%)
    dot_general x32, matrix products, compose(): jnp.einsum('hij,nhjk->nhik', rec_weight, matrix, precision=lax.Precision....  161 us
    pad x32, local copies, waits for them, and re-layouts, shards(): lax.associative_scan(chain_maps, (block_matrix, block_vector))  159 us
    all_gather x8, blocking collectives, prefix_by_axis(): pieces = jax.tree.map(lambda part: lax.all_gather(part, axis), running)  85.8 us
    while x96, local copies, waits for them, and re-layouts  70.3 us
    dot_general x18, matrix products, chain_maps(): jnp.einsum('nhij,nhjk->nhik', later[0], earlier[0], precision=lax.Precisi...  35 us
    dot_general x32, matrix products, advance(): jnp.einsum('hij,nhj->nhi', rec_weight, state, precision=lax.Precision.HIG...  34.9 us
    dot_general x18, matrix products, chain_maps(): jnp.einsum('nhij,nhj->nhi', later[0], earlier[1], precision=lax.Precision...  25 us
    all_gather x1, waiting for transfers between devices, shards(): lax.all_gather(inputs, 'head', axis=1, tiled=True)  24.9 us
  transfers between devices with their start and end apart: 4, of which 4 were waited for; matrix products, arithmetic and copies ran while one was open for 0% of the time, Pallas kernels for 0%

commit v1 on v0

v1 whole, which is shorter than its diff:
```python
import jax
import jax.numpy as jnp
from jax import lax
from jax.experimental import pallas as pl
from jax.experimental.pallas import tpu as pltpu
from jax.sharding import PartitionSpec as P

MESH = pl.DeviceIdType.MESH
F32 = jnp.float32
BF16 = jnp.bfloat16
U = 128
L = 16
B = 32
GB = 8
NG = B // GB
R = GB * L
T = B * L
PAD = 8
M = U + 16
NX = 4
NY = 4
NZ = 4


def split(value):
    high = value.astype(BF16)
    low = (value - high.astype(F32)).astype(BF16)
    return high, low


def pair(value):
    return jnp.concatenate(split(value), axis=1)


def folded(product):
    return product[:, :U] + product[:, U:]


def twice(block):
    return jnp.concatenate([block, block], axis=0)


def dot(a, b):
    return jnp.dot(a, b, preferred_element_type=F32)


def store_pair(ref, rows, value):
    high, low = split(value)
    ref[rows, 0:U] = high
    ref[rows, U : 2 * U] = low


def combine(first, later, out):
    matrix = later[0:U, :]
    product = folded(dot(first[...], twice(matrix)))
    vector = later[U:M, 0:U].astype(F32) + later[U:M, U : 2 * U].astype(F32)
    store_pair(out, pl.ds(0, U), product[0:U])
    store_pair(out, pl.ds(U, M - U), product[U:M] + vector)


def apply_map(state, ref):
    vector = ref[U:M, 0:U].astype(F32) + ref[U:M, U : 2 * U].astype(F32)
    return folded(dot(pair(state), twice(ref[0:U, :]))) + vector


def kernel(
    x_ref, inw_ref, rec_ref, bias_ref, init_ref, guess_ref,
    traj_ref, next_ref,
    xg, inw, wc, cur, drive, slope, offset, work, leaf, node1, node2, node3, node4, mx, my, half, edge, fill,
    local_sem, xs_sem, xr_sem, mxs_sem, mxr_sem, mys_sem, myr_sem, es_sem, er_sem, ns_sem, nr_sem,
):
    tm = lax.axis_index("tm")
    hd = lax.axis_index("head")
    my_x = lax.rem(tm, NX)
    my_y = tm // NX
    my_z = hd // 2
    core = lax.rem(hd, 2)
    turn = 1 - 2 * core
    partner = my_z * 2 + 1 - core
    ahead_z = lax.rem(my_z + turn + NZ, NZ) * 2 + core
    back_z = lax.rem(my_z - turn + NZ, NZ) * 2 + core
    far_z = lax.rem(my_z + 2, NZ) * 2 + core

    def remote(src, dst, ssem, rsem, to):
        return pltpu.make_async_remote_copy(
            src_ref=src, dst_ref=dst, send_sem=ssem, recv_sem=rsem, device_id=to, device_id_type=MESH
        )

    guess_in = [
        pltpu.make_async_copy(
            guess_ref.at[:, pl.ds(h * U, U)], cur.at[h, pl.ds(PAD, T)], local_sem.at[h]
        )
        for h in range(2)
    ]
    weight_in = pltpu.make_async_copy(inw_ref, inw, local_sem.at[2])
    own_in = pltpu.make_async_copy(x_ref, xg.at[hd], local_sem.at[3])
    own_in.start()
    weight_in.start()
    for copy in guess_in:
        copy.start()

    barrier = pltpu.get_barrier_semaphore()

    def greet(a, b):
        pl.semaphore_signal(barrier, inc=1, device_id=(a, b), device_id_type=MESH)

    greet(tm, partner)
    greet(tm, ahead_z)
    greet(tm, back_z)
    for k in range(1, NX):
        greet(my_y * NX + lax.rem(my_x + k, NX), hd)
    for k in range(1, NY):
        greet(lax.rem(my_y + k, NY) * NX + my_x, hd)
    turns_up = jnp.logical_and(my_x == NX - 1, my_y < NY - 1)
    turns_down = jnp.logical_and(my_x == 0, my_y > 0)

    @pl.when(turns_up)
    def _():
        greet(tm + 1, hd)

    @pl.when(turns_down)
    def _():
        greet(tm - 1, hd)

    turning = jnp.logical_or(turns_up, turns_down).astype(jnp.int32)
    pl.semaphore_wait(barrier, 3 + NX - 1 + NY - 1 + turning)

    def chunk_of(g):
        return pl.ds(pl.multiple_of(g * R, R), R)

    def own_chunk(g, kind, to):
        rows = chunk_of(g)
        return remote(
            x_ref.at[rows], xg.at[hd, rows], xs_sem.at[kind, g], xr_sem.at[hd, g], (tm, to)
        )

    def held_chunk(g, kind, source, to):
        rows = chunk_of(g)
        return remote(
            xg.at[source, rows], xg.at[source, rows], xs_sem.at[kind, g], xr_sem.at[source, g], (tm, to)
        )

    def start_own(g, carry):
        own_chunk(g, 0, ahead_z).start()
        own_chunk(g, 1, back_z).start()
        own_chunk(g, 2, partner).start()
        return carry

    lax.fori_loop(0, NG, start_own, 0)

    edge_copy = remote(
        guess_ref.at[pl.ds(T - 8, 8), :], edge, es_sem.at[0], er_sem.at[0],
        (lax.rem(tm + 1, NX * NY), hd),
    )

    @pl.when(tm < NX * NY - 1)
    def _():
        edge_copy.start()

    for h in range(2):
        transposed = rec_ref[h].T
        high, low = split(transposed)
        for k in range(2):
            wc[h, pl.ds(k * U, U), 0:U] = high
            wc[h, pl.ds(k * U, U), U : 2 * U] = low

    for copy in guess_in:
        copy.wait()

    @pl.when(tm == 0)
    def _():
        for h in range(2):
            cur[h, PAD - 1 : PAD, :] = init_ref[h : h + 1, :]

    @pl.when(tm > 0)
    def _():
        edge_copy.wait_recv()
        for h in range(2):
            cur[h, PAD - 1 : PAD, :] = edge[7:8, h * U : (h + 1) * U]

    own_in.wait()
    weight_in.wait()

    def gather_chunk(g):
        held_chunk(g, 3, back_z, ahead_z).wait_recv()
        held_chunk(g, 3, back_z, ahead_z).start()
        held_chunk(g, 4, back_z, partner).start()
        held_chunk(g, 5, ahead_z, partner).wait_recv()
        held_chunk(g, 5, ahead_z, partner).start()
        held_chunk(g, 6, far_z, partner).wait_recv()
        held_chunk(g, 6, far_z, partner).start()
        for z in range(NZ):
            source = z * 2 + 1 - core
            held_chunk(g, 2, source, partner).wait_recv()
        rows = chunk_of(g)
        total = dot(xg[0, rows, :], inw[0 : 2 * U, :])
        for s in range(1, 2 * NZ):
            total += dot(xg[s, rows, :], inw[s * 2 * U : (s + 1) * 2 * U, :])
        for h in range(2):
            drive[h, rows, :] = total[:, h * U : (h + 1) * U] + bias_ref[h : h + 1, :]

    def compose(h, g):
        base = pl.multiple_of(g * R, R)
        weight = wc[h]
        prior = cur[h, pl.ds(base + (PAD - 1), R), :]
        linear = folded(dot(pair(prior), weight))
        value = jnp.tanh(linear + drive[h, pl.ds(base, R), :])
        steep = 1.0 - value * value
        slope[h, pl.ds(base, R), :] = steep
        offset[h, pl.ds(base, R), :] = value - steep * linear
        transposed = rec_ref[h].T
        for b in range(GB):
            row = slope[h, pl.ds(base + b * L, 1), :]
            store_pair(work.at[b], pl.ds(0, U), transposed * row)
        vector = offset[h, pl.ds(base, GB, stride=L), :]
        for step in range(1, L):
            for b in range(GB):
                row = slope[h, pl.ds(base + b * L + step, 1), :]
                product = folded(dot(work[b], weight)) * row
                out = leaf.at[h, g * GB + b] if step == L - 1 else work.at[b]
                store_pair(out, pl.ds(0, U), product)
            wide = folded(dot(pair(twice(vector)), weight))[0:GB]
            vector = wide * slope[h, pl.ds(base + step, GB, stride=L), :]
            vector = vector + offset[h, pl.ds(base + step, GB, stride=L), :]
        for b in range(GB):
            repeated = jnp.broadcast_to(vector[b : b + 1, :], (M - U, U))
            store_pair(leaf.at[h, g * GB + b], pl.ds(U, M - U), repeated)
        for k in range(4):
            combine(leaf.at[h, g * 8 + 2 * k], leaf.at[h, g * 8 + 2 * k + 1], node1.at[h, g * 4 + k])
        for k in range(2):
            combine(node1.at[h, g * 4 + 2 * k], node1.at[h, g * 4 + 2 * k + 1], node2.at[h, g * 2 + k])
        combine(node2.at[h, g * 2], node2.at[h, g * 2 + 1], node3.at[h, g])

    def row_copy(unit, k):
        return remote(
            mx.at[unit, my_x], mx.at[unit, my_x], mxs_sem.at[unit, k], mxr_sem.at[unit, my_x],
            (my_y * NX + lax.rem(my_x + k, NX), hd),
        )

    def row_arrival(unit, k):
        other = lax.rem(my_x + k, NX)
        return remote(
            mx.at[unit, other], mx.at[unit, other], mxs_sem.at[unit, k], mxr_sem.at[unit, other],
            (my_y * NX + other, hd),
        )

    def column_copy(unit, y):
        return remote(
            my.at[unit, my_y], my.at[unit, my_y], mys_sem.at[unit, y], myr_sem.at[unit, my_y],
            (y * NX + my_x, hd),
        )

    def column_arrival(unit, y):
        return remote(
            my.at[unit, y], my.at[unit, y], mys_sem.at[unit, y], myr_sem.at[unit, y],
            (y * NX + my_x, hd),
        )

    def close_slab(h, unit):
        for k in range(2):
            combine(node3.at[h, 2 * k], node3.at[h, 2 * k + 1], node4.at[h, k])
        combine(node4.at[h, 0], node4.at[h, 1], mx.at[unit, my_x])
        for k in range(1, NX):
            row_copy(unit, k).start()

    def exchange_rows(unit):
        for k in range(1, NX):
            row_arrival(unit, k).wait_recv()
        combine(mx.at[unit, 0], mx.at[unit, 1], half.at[0])
        combine(mx.at[unit, 2], mx.at[unit, 3], half.at[1])
        combine(half.at[0], half.at[1], my.at[unit, my_y])
        for y in range(1, NY):

            @pl.when(my_y < y)
            def _():
                column_copy(unit, y).start()

    def finish(h, unit):
        for y in range(NY - 1):

            @pl.when(my_y > y)
            def _():
                column_arrival(unit, y).wait_recv()

        fill[0:16, :] = jnp.broadcast_to(init_ref[pl.ds(h, 1), :], (16, U))
        for y in range(NY - 1):

            @pl.when(my_y > y)
            def _():
                fill[0:16, :] = apply_map(fill[0:16, :], my.at[unit, y])

        for x in range(NX - 1):

            @pl.when(my_x > x)
            def _():
                fill[0:16, :] = apply_map(fill[0:16, :], mx.at[unit, x])

        entering = fill[0:16, :]
        cur[h, PAD - 1 : PAD, :] = entering[0:1]
        starts = [entering]
        for level, node in ((2, node4), (4, node3), (8, node2), (16, node1), (32, leaf)):
            later = []
            for k in range(level // 2):
                later.append(starts[k])
                later.append(apply_map(starts[k], node.at[h, 2 * k]))
            starts = later
        state = jnp.concatenate([one[0:1] for one in starts], axis=0)
        weight = wc[h]
        for step in range(L):
            linear = folded(dot(pair(state), weight))
            state = linear * slope[h, pl.ds(step, B, stride=L), :]
            state = state + offset[h, pl.ds(step, B, stride=L), :]
            cur[h, pl.ds(PAD + step, B, stride=L), :] = state

    def unit_step(u, carry):
        sweep = u // 8
        h = lax.rem(u // 4, 2)
        g = lax.rem(u, 4)

        @pl.when(u < 4)
        def _():
            gather_chunk(g)

        @pl.when(jnp.logical_and(g == 0, u >= 8))
        def _():
            finish(h, h)

        for unit, place in ((0, 6), (1, 9), (2, 13)):

            @pl.when(u == place)
            def _():
                exchange_rows(unit)

        compose(h, g)

        @pl.when(g == NG - 1)
        def _():
            close_slab(h, sweep * 2 + h)

        return carry

    lax.fori_loop(0, 16, unit_step, 0)

    def out_copy(h):
        return pltpu.make_async_copy(
            cur.at[h, pl.ds(PAD, T)], traj_ref.at[:, pl.ds(h * U, U)], local_sem.at[h]
        )

    def next_copy(h):
        return remote(
            cur.at[h, pl.ds(PAD, T)], next_ref.at[:, pl.ds(h * U, U)], ns_sem.at[h], nr_sem.at[h],
            (lax.rem(tm + NX * NY - 1, NX * NY), hd),
        )

    def fill_copy(h):
        return pltpu.make_async_copy(
            fill.at[pl.ds(0, T)], next_ref.at[:, pl.ds(h * U, U)], local_sem.at[2 + h]
        )

    for h in range(2):
        finish(h, 2 + h)
        out_copy(h).start()

        @pl.when(tm > 0)
        def _():
            next_copy(h).start()

        if h == 0:
            exchange_rows(3)

    @pl.when(tm == NX * NY - 1)
    def _():
        for h in range(2):
            fill[...] = jnp.broadcast_to(cur[h, PAD + T - 1 : PAD + T, :], (T, U))
            fill_copy(h).start()
            fill_copy(h).wait()

    def drain(g, carry):
        for kind, to in ((0, ahead_z), (1, back_z), (2, partner)):
            own_chunk(g, kind, to).wait_send()
        held_chunk(g, 3, back_z, ahead_z).wait_send()
        for kind, source in ((4, back_z), (5, ahead_z), (6, far_z)):
            held_chunk(g, kind, source, partner).wait_send()
        return carry

    lax.fori_loop(0, NG, drain, 0)

    @pl.when(tm < NX * NY - 1)
    def _():
        edge_copy.wait_send()

    for unit in range(4):
        for k in range(1, NX):
            row_copy(unit, k).wait_send()
        for y in range(1, NY):

            @pl.when(my_y < y)
            def _():
                column_copy(unit, y).wait_send()

    for h in range(2):
        out_copy(h).wait()

        @pl.when(tm > 0)
        def _():
            next_copy(h).wait_send()

        @pl.when(tm < NX * NY - 1)
        def _():
            next_copy(h).wait_recv()


def shards(inputs, in_weight, rec_weight, bias, initial, guess):
    vmem = pl.BlockSpec(memory_space=pltpu.VMEM)
    anywhere = pl.BlockSpec(memory_space=pl.ANY)
    out = jax.ShapeDtypeStruct((T, 2 * U), F32)
    dma = pltpu.SemaphoreType.DMA
    return pl.pallas_call(
        kernel,
        out_shape=(out, out),
        in_specs=[anywhere, anywhere, vmem, vmem, vmem, anywhere],
        out_specs=(anywhere, anywhere),
        scratch_shapes=[
            pltpu.VMEM((2 * NZ, T, 2 * U), BF16),
            pltpu.VMEM((2 * NZ * 2 * U, 2 * U), BF16),
            pltpu.VMEM((2, 2 * U, 2 * U), BF16),
            pltpu.VMEM((2, PAD + T, U), F32),
            pltpu.VMEM((2, T, U), F32),
            pltpu.VMEM((2, T, U), F32),
            pltpu.VMEM((2, T, U), F32),
            pltpu.VMEM((GB, U, 2 * U), BF16),
            pltpu.VMEM((2, B, M, 2 * U), BF16),
            pltpu.VMEM((2, 16, M, 2 * U), BF16),
            pltpu.VMEM((2, 8, M, 2 * U), BF16),
            pltpu.VMEM((2, 4, M, 2 * U), BF16),
            pltpu.VMEM((2, 2, M, 2 * U), BF16),
            pltpu.VMEM((4, NX, M, 2 * U), BF16),
            pltpu.VMEM((4, NY, M, 2 * U), BF16),
            pltpu.VMEM((2, M, 2 * U), BF16),
            pltpu.VMEM((8, 2 * U), F32),
            pltpu.VMEM((T, U), F32),
            dma((4,)),
            dma((7, NG)),
            dma((2 * NZ, NG)),
            dma((4, NX)),
            dma((4, NX)),
            dma((4, NY)),
            dma((4, NY)),
            dma((1,)),
            dma((1,)),
            dma((2,)),
            dma((2,)),
        ],
        compiler_params=pltpu.CompilerParams(
            collective_id=0, has_side_effects=True, vmem_limit_bytes=56 * 1024 * 1024
        ),
    )(
        inputs,
        in_weight,
        rec_weight,
        bias.reshape(2, U),
        initial.reshape(2, U),
        guess,
    )


def solution(mesh):
    in_specs = (
        P("tm", "head"),
        P(None, "head"),
        P("head", None, None),
        P("head"),
        P("head"),
        P("tm", "head"),
    )
    out_specs = (P("tm", "head"), P("tm", "head"))
    return jax.shard_map(
        shards, mesh=mesh, in_specs=in_specs, out_specs=out_specs, check_vma=False
    )
```

time: 823 us -> 122 us (0.15)
  the two profiles are of different devices: /device:TPU:6 before, /device:TPU:22 now
where the time goes in v1:
time: 122 us; the launch traced here: 120 us
  Pallas kernels  117 us (96%)
  local copies, waits for them, and re-layouts  2.72 us (2%)
    pallas_call x1, Pallas kernels, shards(): pl.pallas_call(kernel, out_shape=(out, out), in_specs=[anywhere, anywhere...  117 us
    unnamed x4, local copies, waits for them, and re-layouts  2.72 us

profile of v1, /device:TPU:22, one launch (start us, length us, event | category | flops | bytes accessed | tf_op | source)
XLA Modules:
  0.0 119.9 jit_solution(11109522553463518762)
XLA Ops:
  0.6 116.5 %shard_map.77 = (f32[512,256]{1,0:T(8,128)}, f32[512,256]{1,0:T(8,128)}) custom-call(bf16[512,256]{1,0:T(8,128)(2,1)} %x_ref.1, bf16[2048,256]{1,0:T(8,128)(2,1)} %inw_ref.1, f32[2,128,128]{2,1,0:T(8,128)} %rec_ref.1, f32[2,128]{1,0:T(2,128)} %bitcast.2, f32[2,128]{1,0:T(2,128)} %bitcast.3, f32[512,256]{1,0:T(8,128)} %guess_ref.1), custom_call_target="tpu_custom_call" | custom-call | tf_op jit(solution)/shard_map/pallas_call | solution.py:418
  117.2 0.0 copy-start
  117.2 1.9 %copy.10 = f32[512,256]{1,0:T(8,128)} copy(f32[512,256]{1,0:T(8,128)} %get-tuple-element.4) | data formatting | bytes 1048576
  119.1 0.0 copy-done
  119.1 0.8 copy.11
Async XLA Ops:
  117.2 1.9 %copy-start = (f32[512,256]{1,0:T(8,128)S(1)}, f32[512,256]{1,0:T(8,128)}, u32[]{:S(2)}) copy-start(f32[512,256]{1,0:T(8,128)} %get-tuple-element.5) | copy-start | bytes 1572868

commit v2 on v1

--- a/solution.py
+++ b/solution.py
@@ -9,12 +9,13 @@
 F32 = jnp.float32
 BF16 = jnp.bfloat16
 U = 128
+NB = 8
+NG = 4
 L = 16
-B = 32
-GB = 8
-NG = B // GB
-R = GB * L
-T = B * L
+S = NG * L
+R = NB * L
+B = NB * NG
+T = NB * S
 PAD = 8
 M = U + 16
 NX = 4
@@ -64,9 +65,9 @@
 
 
 def kernel(
-    x_ref, inw_ref, rec_ref, bias_ref, init_ref, guess_ref,
+    x_ref, inw_ref, rec_hbm, bias_hbm, init_hbm, guess_ref,
     traj_ref, next_ref,
-    xg, inw, wc, cur, drive, slope, offset, work, leaf, node1, node2, node3, node4, mx, my, half, edge, fill,
+    rec_ref, bias_ref, init_ref, xg, inw, wc, cur, drive, slope, offset, work, leaf, node1, node2, vec, mx, whole, entry, leaving, half, edge, fill,
     local_sem, xs_sem, xr_sem, mxs_sem, mxr_sem, mys_sem, myr_sem, es_sem, er_sem, ns_sem, nr_sem,
 ):
     tm = lax.axis_index("tm")
@@ -94,6 +95,14 @@
     ]
     weight_in = pltpu.make_async_copy(inw_ref, inw, local_sem.at[2])
     own_in = pltpu.make_async_copy(x_ref, xg.at[hd], local_sem.at[3])
+    small_in = [
+        pltpu.make_async_copy(src, dst, local_sem.at[4 + k])
+        for k, (src, dst) in enumerate(
+            ((rec_hbm, rec_ref), (bias_hbm, bias_ref), (init_hbm, init_ref))
+        )
+    ]
+    for copy in small_in:
+        copy.start()
     own_in.start()
     weight_in.start()
     for copy in guess_in:
@@ -126,27 +135,27 @@
     pl.semaphore_wait(barrier, 3 + NX - 1 + NY - 1 + turning)
 
     def chunk_of(g):
-        return pl.ds(pl.multiple_of(g * R, R), R)
+        return pl.ds(pl.multiple_of(g * L, L), L)
 
     def own_chunk(g, kind, to):
         rows = chunk_of(g)
         return remote(
-            x_ref.at[rows], xg.at[hd, rows], xs_sem.at[kind, g], xr_sem.at[hd, g], (tm, to)
+            x_ref.at[:, rows], xg.at[hd, :, rows], xs_sem.at[kind, g], xr_sem.at[hd, g], (tm, to)
         )
 
     def held_chunk(g, kind, source, to):
         rows = chunk_of(g)
         return remote(
-            xg.at[source, rows], xg.at[source, rows], xs_sem.at[kind, g], xr_sem.at[source, g], (tm, to)
-        )
-
-    def start_own(g, carry):
+            xg.at[source, :, rows], xg.at[source, :, rows], xs_sem.at[kind, g], xr_sem.at[source, g], (tm, to)
+        )
+
+    def start_own(g):
         own_chunk(g, 0, ahead_z).start()
         own_chunk(g, 1, back_z).start()
         own_chunk(g, 2, partner).start()
-        return carry
-
-    lax.fori_loop(0, NG, start_own, 0)
+
+    start_own(0)
+    start_own(1)
 
     edge_copy = remote(
         guess_ref.at[pl.ds(T - 8, 8), :], edge, es_sem.at[0], er_sem.at[0],
@@ -156,6 +165,9 @@
     @pl.when(tm < NX * NY - 1)
     def _():
         edge_copy.start()
+
+    for copy in small_in:
+        copy.wait()
 
     for h in range(2):
         transposed = rec_ref[h].T
@@ -164,6 +176,12 @@
             wc[h, pl.ds(k * U, U), 0:U] = high
             wc[h, pl.ds(k * U, U), U : 2 * U] = low
 
+    row_id = lax.broadcasted_iota(jnp.int32, (U, U), 0)
+    identity = jnp.where(row_id == lax.broadcasted_iota(jnp.int32, (U, U), 1), 1.0, 0.0)
+    for h in range(2):
+        for b in range(NB):
+            store_pair(leaf.at[h, 0, b], pl.ds(0, U), identity)
+
     for copy in guess_in:
         copy.wait()
 
@@ -181,55 +199,84 @@
     own_in.wait()
     weight_in.wait()
 
-    def gather_chunk(g):
+    def relay_chunk(g):
         held_chunk(g, 3, back_z, ahead_z).wait_recv()
         held_chunk(g, 3, back_z, ahead_z).start()
         held_chunk(g, 4, back_z, partner).start()
         held_chunk(g, 5, ahead_z, partner).wait_recv()
         held_chunk(g, 5, ahead_z, partner).start()
+
+    def far_chunk(g):
         held_chunk(g, 6, far_z, partner).wait_recv()
         held_chunk(g, 6, far_z, partner).start()
+
+    def curve(h, starts, rows, linear):
+        through = jnp.concatenate([drive[h, pl.ds(t, rows), :] for t in starts], axis=0)
+        value = jnp.tanh(linear + through)
+        steep = 1.0 - value * value
+        rest = value - steep * linear
+        for k, t in enumerate(starts):
+            slope[h, pl.ds(t, rows), :] = steep[k * rows : (k + 1) * rows]
+            offset[h, pl.ds(t, rows), :] = rest[k * rows : (k + 1) * rows]
+
+    def linear_of(h, starts, rows):
+        prior = jnp.concatenate([cur[h, pl.ds(t + (PAD - 1), rows), :] for t in starts], axis=0)
+        return folded(dot(pair(prior), wc[h]))
+
+    def gather_chunk(g):
+        @pl.when(g == 0)
+        def _():
+            relay_chunk(0)
+            start_own(2)
+            far_chunk(0)
+            relay_chunk(1)
+
+        @pl.when(g > 0)
+        def _():
+            far_chunk(g)
+
+        @pl.when(jnp.logical_and(g > 0, g < NG - 1))
+        def _():
+            relay_chunk(g + 1)
+
+        @pl.when(g == 1)
+        def _():
+            start_own(3)
+
+        first = pl.multiple_of(g * L, L)
+        starts = [first + b * S for b in range(NB)]
+        linear = [linear_of(h, starts, L) for h in range(2)]
         for z in range(NZ):
             source = z * 2 + 1 - core
             held_chunk(g, 2, source, partner).wait_recv()
         rows = chunk_of(g)
-        total = dot(xg[0, rows, :], inw[0 : 2 * U, :])
-        for s in range(1, 2 * NZ):
-            total += dot(xg[s, rows, :], inw[s * 2 * U : (s + 1) * 2 * U, :])
+        total = jnp.zeros((R, 2 * U), F32)
+        for s in range(2 * NZ):
+            total += dot(xg[s, :, rows, :].reshape(R, 2 * U), inw[s * 2 * U : (s + 1) * 2 * U, :])
         for h in range(2):
-            drive[h, rows, :] = total[:, h * U : (h + 1) * U] + bias_ref[h : h + 1, :]
+            through = total[:, h * U : (h + 1) * U] + bias_ref[h : h + 1, :]
+            for k, t in enumerate(starts):
+                drive[h, pl.ds(t, L), :] = through[k * L : (k + 1) * L]
+            curve(h, starts, L, linear[h])
 
     def compose(h, g):
-        base = pl.multiple_of(g * R, R)
+        first = pl.multiple_of(g * L, L)
         weight = wc[h]
-        prior = cur[h, pl.ds(base + (PAD - 1), R), :]
-        linear = folded(dot(pair(prior), weight))
-        value = jnp.tanh(linear + drive[h, pl.ds(base, R), :])
-        steep = 1.0 - value * value
-        slope[h, pl.ds(base, R), :] = steep
-        offset[h, pl.ds(base, R), :] = value - steep * linear
-        transposed = rec_ref[h].T
-        for b in range(GB):
-            row = slope[h, pl.ds(base + b * L, 1), :]
-            store_pair(work.at[b], pl.ds(0, U), transposed * row)
-        vector = offset[h, pl.ds(base, GB, stride=L), :]
-        for step in range(1, L):
-            for b in range(GB):
-                row = slope[h, pl.ds(base + b * L + step, 1), :]
-                product = folded(dot(work[b], weight)) * row
-                out = leaf.at[h, g * GB + b] if step == L - 1 else work.at[b]
+        vector = jnp.where(g == 0, 0.0, vec[h])
+        for step in range(L):
+            for b in range(NB):
+                row = slope[h, pl.ds(first + (b * S + step), 1), :]
+                block = leaf.at[h, g, b] if step == 0 else work.at[b]
+                product = folded(dot(block[0:U, :], weight)) * row
+                out = leaf.at[h, g + 1, b] if step == L - 1 else work.at[b]
                 store_pair(out, pl.ds(0, U), product)
-            wide = folded(dot(pair(twice(vector)), weight))[0:GB]
-            vector = wide * slope[h, pl.ds(base + step, GB, stride=L), :]
-            vector = vector + offset[h, pl.ds(base + step, GB, stride=L), :]
-        for b in range(GB):
+            wide = folded(dot(pair(twice(vector)), weight))[0:NB]
+            vector = wide * slope[h, pl.ds(first + step, NB, stride=S), :]
+            vector = vector + offset[h, pl.ds(first + step, NB, stride=S), :]
+        vec[h] = vector
+        for b in range(NB):
             repeated = jnp.broadcast_to(vector[b : b + 1, :], (M - U, U))
-            store_pair(leaf.at[h, g * GB + b], pl.ds(U, M - U), repeated)
-        for k in range(4):
-            combine(leaf.at[h, g * 8 + 2 * k], leaf.at[h, g * 8 + 2 * k + 1], node1.at[h, g * 4 + k])
-        for k in range(2):
-            combine(node1.at[h, g * 4 + 2 * k], node1.at[h, g * 4 + 2 * k + 1], node2.at[h, g * 2 + k])
-        combine(node2.at[h, g * 2], node2.at[h, g * 2 + 1], node3.at[h, g])
+            store_pair(leaf.at[h, g + 1, b], pl.ds(U, M - U), repeated)
 
     def row_copy(unit, k):
         return remote(
@@ -244,51 +291,44 @@
             (my_y * NX + other, hd),
         )
 
-    def column_copy(unit, y):
+    def state_copy(unit, y):
         return remote(
-            my.at[unit, my_y], my.at[unit, my_y], mys_sem.at[unit, y], myr_sem.at[unit, my_y],
-            (y * NX + my_x, hd),
-        )
-
-    def column_arrival(unit, y):
-        return remote(
-            my.at[unit, y], my.at[unit, y], mys_sem.at[unit, y], myr_sem.at[unit, y],
-            (y * NX + my_x, hd),
+            leaving.at[unit], entry.at[unit], mys_sem.at[unit], myr_sem.at[unit],
+            (lax.rem(y + 1, NY) * NX + my_x, hd),
         )
 
     def close_slab(h, unit):
+        for k in range(4):
+            combine(leaf.at[h, NG, 2 * k], leaf.at[h, NG, 2 * k + 1], node1.at[h, k])
         for k in range(2):
-            combine(node3.at[h, 2 * k], node3.at[h, 2 * k + 1], node4.at[h, k])
-        combine(node4.at[h, 0], node4.at[h, 1], mx.at[unit, my_x])
+            combine(node1.at[h, 2 * k], node1.at[h, 2 * k + 1], node2.at[h, k])
+        combine(node2.at[h, 0], node2.at[h, 1], mx.at[unit, my_x])
         for k in range(1, NX):
             row_copy(unit, k).start()
 
-    def exchange_rows(unit):
+    def close_row(unit):
         for k in range(1, NX):
             row_arrival(unit, k).wait_recv()
         combine(mx.at[unit, 0], mx.at[unit, 1], half.at[0])
         combine(mx.at[unit, 2], mx.at[unit, 3], half.at[1])
-        combine(half.at[0], half.at[1], my.at[unit, my_y])
-        for y in range(1, NY):
-
-            @pl.when(my_y < y)
-            def _():
-                column_copy(unit, y).start()
+        combine(half.at[0], half.at[1], whole)
+
+    def pass_row(h, unit, y):
+        @pl.when(my_y == y)
+        def _():
+            if y == 0:
+                entry[unit] = jnp.broadcast_to(init_ref[h : h + 1, :], (16, U))
+            else:
+                state_copy(unit, y).wait_recv()
+            leaving[unit] = apply_map(entry[unit], whole)
+            state_copy(unit, y).start()
 
     def finish(h, unit):
-        for y in range(NY - 1):
-
-            @pl.when(my_y > y)
-            def _():
-                column_arrival(unit, y).wait_recv()
-
-        fill[0:16, :] = jnp.broadcast_to(init_ref[pl.ds(h, 1), :], (16, U))
-        for y in range(NY - 1):
-
-            @pl.when(my_y > y)
-            def _():
-                fill[0:16, :] = apply_map(fill[0:16, :], my.at[unit, y])
-
+        @pl.when(my_y == NY - 1)
+        def _():
+            state_copy(unit, NY - 1).wait_recv()
+
+        fill[0:16, :] = entry[unit]
         for x in range(NX - 1):
 
             @pl.when(my_x > x)
@@ -298,13 +338,18 @@
         entering = fill[0:16, :]
         cur[h, PAD - 1 : PAD, :] = entering[0:1]
         starts = [entering]
-        for level, node in ((2, node4), (4, node3), (8, node2), (16, node1), (32, leaf)):
+        for node in (node2.at[h], node1.at[h], leaf.at[h, NG]):
             later = []
-            for k in range(level // 2):
+            for k in range(len(starts)):
                 later.append(starts[k])
-                later.append(apply_map(starts[k], node.at[h, 2 * k]))
+                later.append(apply_map(starts[k], node.at[2 * k]))
             starts = later
-        state = jnp.concatenate([one[0:1] for one in starts], axis=0)
+        states = []
+        for b in range(NB):
+            states.append(starts[b][0:1])
+            for g in range(1, NG):
+                states.append(apply_map(starts[b], leaf.at[h, g, b])[0:1])
+        state = jnp.concatenate(states, axis=0)
         weight = wc[h]
         for step in range(L):
             linear = folded(dot(pair(state), weight))
@@ -321,15 +366,22 @@
         def _():
             gather_chunk(g)
 
+        for unit, closes, passes in ((0, 7, (7, 8, 8)), (1, 9, (9, 10, 11)), (2, 13, (13, 14, 15))):
+
+            @pl.when(u == closes)
+            def _():
+                close_row(unit)
+
+            for y in range(NY - 1):
+
+                @pl.when(u == passes[y])
+                def _():
+                    pass_row(unit % 2, unit, y)
+
         @pl.when(jnp.logical_and(g == 0, u >= 8))
         def _():
             finish(h, h)
-
-        for unit, place in ((0, 6), (1, 9), (2, 13)):
-
-            @pl.when(u == place)
-            def _():
-                exchange_rows(unit)
+            curve(h, [0], T, linear_of(h, [0], T))
 
         compose(h, g)
 
@@ -366,7 +418,9 @@
             next_copy(h).start()
 
         if h == 0:
-            exchange_rows(3)
+            close_row(3)
+            for y in range(NY - 1):
+                pass_row(1, 3, y)
 
     @pl.when(tm == NX * NY - 1)
     def _():
@@ -392,11 +446,10 @@
     for unit in range(4):
         for k in range(1, NX):
             row_copy(unit, k).wait_send()
-        for y in range(1, NY):
-
-            @pl.when(my_y < y)
-            def _():
-                column_copy(unit, y).wait_send()
+
+        @pl.when(my_y < NY - 1)
+        def _():
+            state_copy(unit, my_y).wait_send()
 
     for h in range(2):
         out_copy(h).wait()
@@ -411,41 +464,45 @@
 
 
 def shards(inputs, in_weight, rec_weight, bias, initial, guess):
-    vmem = pl.BlockSpec(memory_space=pltpu.VMEM)
+    hbm = pl.BlockSpec(memory_space=pltpu.HBM)
     anywhere = pl.BlockSpec(memory_space=pl.ANY)
     out = jax.ShapeDtypeStruct((T, 2 * U), F32)
     dma = pltpu.SemaphoreType.DMA
     return pl.pallas_call(
         kernel,
         out_shape=(out, out),
-        in_specs=[anywhere, anywhere, vmem, vmem, vmem, anywhere],
+        in_specs=[hbm] * 6,
         out_specs=(anywhere, anywhere),
         scratch_shapes=[
-            pltpu.VMEM((2 * NZ, T, 2 * U), BF16),
+            pltpu.VMEM((2, U, U), F32),
+            pltpu.VMEM((2, U), F32),
+            pltpu.VMEM((2, U), F32),
+            pltpu.VMEM((2 * NZ, NB, S, 2 * U), BF16),
             pltpu.VMEM((2 * NZ * 2 * U, 2 * U), BF16),
             pltpu.VMEM((2, 2 * U, 2 * U), BF16),
             pltpu.VMEM((2, PAD + T, U), F32),
             pltpu.VMEM((2, T, U), F32),
             pltpu.VMEM((2, T, U), F32),
             pltpu.VMEM((2, T, U), F32),
-            pltpu.VMEM((GB, U, 2 * U), BF16),
-            pltpu.VMEM((2, B, M, 2 * U), BF16),
-            pltpu.VMEM((2, 16, M, 2 * U), BF16),
-            pltpu.VMEM((2, 8, M, 2 * U), BF16),
+            pltpu.VMEM((NB, U, 2 * U), BF16),
+            pltpu.VMEM((2, NG + 1, NB, M, 2 * U), BF16),
             pltpu.VMEM((2, 4, M, 2 * U), BF16),
             pltpu.VMEM((2, 2, M, 2 * U), BF16),
+            pltpu.VMEM((2, NB, U), F32),
             pltpu.VMEM((4, NX, M, 2 * U), BF16),
-            pltpu.VMEM((4, NY, M, 2 * U), BF16),
+            pltpu.VMEM((M, 2 * U), BF16),
+            pltpu.VMEM((4, 16, U), F32),
+            pltpu.VMEM((4, 16, U), F32),
             pltpu.VMEM((2, M, 2 * U), BF16),
             pltpu.VMEM((8, 2 * U), F32),
             pltpu.VMEM((T, U), F32),
-            dma((4,)),
+            dma((7,)),
             dma((7, NG)),
             dma((2 * NZ, NG)),
             dma((4, NX)),
             dma((4, NX)),
-            dma((4, NY)),
-            dma((4, NY)),
+            dma((4,)),
+            dma((4,)),
             dma((1,)),
             dma((1,)),
             dma((2,)),
@@ -455,7 +512,7 @@
             collective_id=0, has_side_effects=True, vmem_limit_bytes=56 * 1024 * 1024
         ),
     )(
-        inputs,
+        inputs.reshape(NB, S, 2 * U),
         in_weight,
         rec_weight,
         bias.reshape(2, U),

time: 122 us -> 103 us (0.84); the launches traced: 120 us -> 103 us
  Pallas kernels: 117 us -> 100 us
    pallas_call x1, Pallas kernels: 117 us -> 100 us  [shards(): pl.pallas_call(kernel, out_shape=(out, out), in_specs=[hbm] * 6, out_spec...]
where the time goes in v2:
time: 103 us
  Pallas kernels  100 us (97%)
  local copies, waits for them, and re-layouts  2.72 us (3%)
    pallas_call x1, Pallas kernels, shards(): pl.pallas_call(kernel, out_shape=(out, out), in_specs=[hbm] * 6, out_spec...  100 us
    unnamed x4, local copies, waits for them, and re-layouts  2.72 us

profile of v2, /device:TPU:22, one launch (start us, length us, event | category | flops | bytes accessed | tf_op | source)
XLA Modules:
  0.0 103.4 jit_solution(2345548395902848144)
XLA Ops:
  0.6 100.0 %shard_map.77 = (f32[512,256]{1,0:T(8,128)}, f32[512,256]{1,0:T(8,128)}) custom-call(bf16[8,64,256]{2,1,0:T(8,128)(2,1)} %bitcast.3, bf16[2048,256]{1,0:T(8,128)(2,1)} %inw_ref.1, f32[2,128,128]{2,1,0:T(8,128)} %rec_hbm.1, f32[2,128]{1,0:T(2,128)} %bitcast.4, f32[2,128]{1,0:T(2,128)} %bitcast.5, f32[512,256]{1,0:T(8,128)} %guess_ref.1), custom_call_target="tpu_custom_call" | custom-call | tf_op jit(solution)/shard_map/pallas_call | solution.py:471
  100.6 0.0 copy-start
  100.6 1.9 %copy.10 = f32[512,256]{1,0:T(8,128)} copy(f32[512,256]{1,0:T(8,128)} %get-tuple-element.4) | data formatting | bytes 1048576
  102.6 0.0 copy-done
  102.6 0.8 copy.11
Async XLA Ops:
  100.6 1.9 %copy-start = (f32[512,256]{1,0:T(8,128)S(1)}, f32[512,256]{1,0:T(8,128)}, u32[]{:S(2)}) copy-start(f32[512,256]{1,0:T(8,128)} %get-tuple-element.5) | copy-start | bytes 1572868

commit v3 on v2

--- a/solution.py
+++ b/solution.py
@@ -68,7 +68,9 @@
     x_ref, inw_ref, rec_hbm, bias_hbm, init_hbm, guess_ref,
     traj_ref, next_ref,
     rec_ref, bias_ref, init_ref, xg, inw, wc, cur, drive, slope, offset, work, leaf, node1, node2, vec, mx, whole, entry, leaving, half, edge, fill,
+    ndrive, ncur, nslope, noffset, origin, norigin, ahead,
     local_sem, xs_sem, xr_sem, mxs_sem, mxr_sem, mys_sem, myr_sem, es_sem, er_sem, ns_sem, nr_sem,
+    nds_sem, ndr_sem, ncs_sem, ncr_sem,
 ):
     tm = lax.axis_index("tm")
     hd = lax.axis_index("head")
@@ -81,6 +83,7 @@
     ahead_z = lax.rem(my_z + turn + NZ, NZ) * 2 + core
     back_z = lax.rem(my_z - turn + NZ, NZ) * 2 + core
     far_z = lax.rem(my_z + 2, NZ) * 2 + core
+    across = ahead_z + turn
 
     def remote(src, dst, ssem, rsem, to):
         return pltpu.make_async_remote_copy(
@@ -116,6 +119,7 @@
     greet(tm, partner)
     greet(tm, ahead_z)
     greet(tm, back_z)
+    greet(tm, across)
     for k in range(1, NX):
         greet(my_y * NX + lax.rem(my_x + k, NX), hd)
     for k in range(1, NY):
@@ -132,7 +136,7 @@
         greet(tm - 1, hd)
 
     turning = jnp.logical_or(turns_up, turns_down).astype(jnp.int32)
-    pl.semaphore_wait(barrier, 3 + NX - 1 + NY - 1 + turning)
+    pl.semaphore_wait(barrier, 4 + NX - 1 + NY - 1 + turning)
 
     def chunk_of(g):
         return pl.ds(pl.multiple_of(g * L, L), L)
@@ -202,16 +206,12 @@
     def relay_chunk(g):
         held_chunk(g, 3, back_z, ahead_z).wait_recv()
         held_chunk(g, 3, back_z, ahead_z).start()
+        held_chunk(g, 6, back_z, across).start()
         held_chunk(g, 4, back_z, partner).start()
         held_chunk(g, 5, ahead_z, partner).wait_recv()
         held_chunk(g, 5, ahead_z, partner).start()
 
-    def far_chunk(g):
-        held_chunk(g, 6, far_z, partner).wait_recv()
-        held_chunk(g, 6, far_z, partner).start()
-
-    def curve(h, starts, rows, linear):
-        through = jnp.concatenate([drive[h, pl.ds(t, rows), :] for t in starts], axis=0)
+    def curve(h, starts, rows, linear, through, slope=slope, offset=offset):
         value = jnp.tanh(linear + through)
         steep = 1.0 - value * value
         rest = value - steep * linear
@@ -219,21 +219,31 @@
             slope[h, pl.ds(t, rows), :] = steep[k * rows : (k + 1) * rows]
             offset[h, pl.ds(t, rows), :] = rest[k * rows : (k + 1) * rows]
 
-    def linear_of(h, starts, rows):
+    def linear_of(h, starts, rows, cur=cur):
         prior = jnp.concatenate([cur[h, pl.ds(t + (PAD - 1), rows), :] for t in starts], axis=0)
         return folded(dot(pair(prior), wc[h]))
 
+    previous = (lax.rem(tm + NX * NY - 1, NX * NY), hd)
+
+    def drive_copy(g):
+        rows = chunk_of(g)
+        return remote(
+            drive.at[:, :, rows], ndrive.at[:, :, rows], nds_sem.at[g], ndr_sem.at[g], previous
+        )
+
+    def path_copy(h):
+        steps = pl.ds(PAD, T)
+        return remote(cur.at[h, steps], ncur.at[h, steps], ncs_sem.at[h], ncr_sem.at[h], previous)
+
+    def start_copy(h):
+        return remote(origin.at[h], norigin.at[h], ns_sem.at[h], nr_sem.at[h], previous)
+
     def gather_chunk(g):
         @pl.when(g == 0)
         def _():
             relay_chunk(0)
             start_own(2)
-            far_chunk(0)
             relay_chunk(1)
-
-        @pl.when(g > 0)
-        def _():
-            far_chunk(g)
 
         @pl.when(jnp.logical_and(g > 0, g < NG - 1))
         def _():
@@ -246,6 +256,7 @@
         first = pl.multiple_of(g * L, L)
         starts = [first + b * S for b in range(NB)]
         linear = [linear_of(h, starts, L) for h in range(2)]
+        held_chunk(g, 3, far_z, ahead_z).wait_recv()
         for z in range(NZ):
             source = z * 2 + 1 - core
             held_chunk(g, 2, source, partner).wait_recv()
@@ -255,9 +266,12 @@
             total += dot(xg[s, :, rows, :].reshape(R, 2 * U), inw[s * 2 * U : (s + 1) * 2 * U, :])
         for h in range(2):
             through = total[:, h * U : (h + 1) * U] + bias_ref[h : h + 1, :]
-            for k, t in enumerate(starts):
-                drive[h, pl.ds(t, L), :] = through[k * L : (k + 1) * L]
-            curve(h, starts, L, linear[h])
+            drive[h, :, rows, :] = through.reshape(NB, L, U)
+            curve(h, starts, L, linear[h], through)
+
+        @pl.when(tm > 0)
+        def _():
+            drive_copy(g).start()
 
     def compose(h, g):
         first = pl.multiple_of(g * L, L)
@@ -323,7 +337,7 @@
             leaving[unit] = apply_map(entry[unit], whole)
             state_copy(unit, y).start()
 
-    def finish(h, unit):
+    def finish(h, unit, last=False):
         @pl.when(my_y == NY - 1)
         def _():
             state_copy(unit, NY - 1).wait_recv()
@@ -350,12 +364,23 @@
             for g in range(1, NG):
                 states.append(apply_map(starts[b], leaf.at[h, g, b])[0:1])
         state = jnp.concatenate(states, axis=0)
+        if last:
+            origin[h] = state
+
+            @pl.when(tm > 0)
+            def _():
+                start_copy(h).start()
+                path_copy(h).wait_send()
+
+        advance(h, state, slope, offset, cur, PAD)
+
+    def advance(h, state, slope, offset, out, base):
         weight = wc[h]
         for step in range(L):
             linear = folded(dot(pair(state), weight))
             state = linear * slope[h, pl.ds(step, B, stride=L), :]
             state = state + offset[h, pl.ds(step, B, stride=L), :]
-            cur[h, pl.ds(PAD + step, B, stride=L), :] = state
+            out[h, pl.ds(base + step, B, stride=L), :] = state
 
     def unit_step(u, carry):
         sweep = u // 8
@@ -381,7 +406,13 @@
         @pl.when(jnp.logical_and(g == 0, u >= 8))
         def _():
             finish(h, h)
-            curve(h, [0], T, linear_of(h, [0], T))
+
+            @pl.when(tm > 0)
+            def _():
+                path_copy(h).start()
+
+            ncur[h, PAD - 1 : PAD, :] = cur[h, PAD + T - 1 : PAD + T, :]
+            curve(h, [0], T, linear_of(h, [0], T), drive[h].reshape(T, U))
 
         compose(h, g)
 
@@ -399,41 +430,66 @@
         )
 
     def next_copy(h):
-        return remote(
-            cur.at[h, pl.ds(PAD, T)], next_ref.at[:, pl.ds(h * U, U)], ns_sem.at[h], nr_sem.at[h],
-            (lax.rem(tm + NX * NY - 1, NX * NY), hd),
-        )
-
-    def fill_copy(h):
         return pltpu.make_async_copy(
-            fill.at[pl.ds(0, T)], next_ref.at[:, pl.ds(h * U, U)], local_sem.at[2 + h]
-        )
-
-    for h in range(2):
-        finish(h, 2 + h)
-        out_copy(h).start()
-
-        @pl.when(tm > 0)
-        def _():
-            next_copy(h).start()
-
-        if h == 0:
-            close_row(3)
-            for y in range(NY - 1):
-                pass_row(1, 3, y)
-
-    @pl.when(tm == NX * NY - 1)
-    def _():
-        for h in range(2):
-            fill[...] = jnp.broadcast_to(cur[h, PAD + T - 1 : PAD + T, :], (T, U))
-            fill_copy(h).start()
-            fill_copy(h).wait()
+            ahead.at[h], next_ref.at[:, pl.ds(h * U, U)], local_sem.at[2 + h]
+        )
+
+    def follow(h):
+        @pl.when(tm < NX * NY - 1)
+        def _():
+            start_copy(h).wait_recv()
+            advance(h, norigin[h], nslope, noffset, ahead, 0)
+
+        @pl.when(tm == NX * NY - 1)
+        def _():
+            ahead[h] = jnp.broadcast_to(cur[h, PAD + T - 1 : PAD + T, :], (T, U))
+
+        next_copy(h).start()
+
+    finish(0, 2, last=True)
+    out_copy(0).start()
+
+    def following_curve():
+        @pl.when(tm < NX * NY - 1)
+        def _():
+            for g in range(NG):
+                drive_copy(g).wait_recv()
+            for h in range(2):
+                path_copy(h).wait_recv()
+                linear = linear_of(h, [0], T, ncur)
+                curve(h, [0], T, linear, ndrive[h].reshape(T, U), nslope, noffset)
+
+    close_row(3)
+
+    @pl.when(my_y > 0)
+    def _():
+        following_curve()
+
+    @pl.when(my_y >= 2)
+    def _():
+        follow(0)
+
+    for y in range(NY - 1):
+        pass_row(1, 3, y)
+
+    @pl.when(my_y == 0)
+    def _():
+        following_curve()
+
+    @pl.when(my_y < 2)
+    def _():
+        follow(0)
+
+    finish(1, 3, last=True)
+    out_copy(1).start()
+    follow(1)
 
     def drain(g, carry):
         for kind, to in ((0, ahead_z), (1, back_z), (2, partner)):
             own_chunk(g, kind, to).wait_send()
         held_chunk(g, 3, back_z, ahead_z).wait_send()
-        for kind, source in ((4, back_z), (5, ahead_z), (6, far_z)):
+        held_chunk(g, 6, back_z, across).wait_send()
+        for kind, source in ((4, back_z), (5, ahead_z)):
             held_chunk(g, kind, source, partner).wait_send()
         return carry
 
@@ -451,16 +507,16 @@
         def _():
             state_copy(unit, my_y).wait_send()
 
+    @pl.when(tm > 0)
+    def _():
+        for g in range(NG):
+            drive_copy(g).wait_send()
+        for h in range(2):
+            start_copy(h).wait_send()
+
     for h in range(2):
         out_copy(h).wait()
-
-        @pl.when(tm > 0)
-        def _():
-            next_copy(h).wait_send()
-
-        @pl.when(tm < NX * NY - 1)
-        def _():
-            next_copy(h).wait_recv()
+        next_copy(h).wait()
 
 
 def shards(inputs, in_weight, rec_weight, bias, initial, guess):
@@ -481,7 +537,7 @@
             pltpu.VMEM((2 * NZ * 2 * U, 2 * U), BF16),
             pltpu.VMEM((2, 2 * U, 2 * U), BF16),
             pltpu.VMEM((2, PAD + T, U), F32),
-            pltpu.VMEM((2, T, U), F32),
+            pltpu.VMEM((2, NB, S, U), F32),
             pltpu.VMEM((2, T, U), F32),
             pltpu.VMEM((2, T, U), F32),
             pltpu.VMEM((NB, U, 2 * U), BF16),
@@ -495,7 +551,14 @@
             pltpu.VMEM((4, 16, U), F32),
             pltpu.VMEM((2, M, 2 * U), BF16),
             pltpu.VMEM((8, 2 * U), F32),
-            pltpu.VMEM((T, U), F32),
+            pltpu.VMEM((16, U), F32),
+            pltpu.VMEM((2, NB, S, U), F32),
+            pltpu.VMEM((2, PAD + T, U), F32),
+            pltpu.VMEM((2, T, U), F32),
+            pltpu.VMEM((2, T, U), F32),
+            pltpu.VMEM((2, B, U), F32),
+            pltpu.VMEM((2, B, U), F32),
+            pltpu.VMEM((2, T, U), F32),
             dma((7,)),
             dma((7, NG)),
             dma((2 * NZ, NG)),
@@ -505,6 +568,10 @@
             dma((4,)),
             dma((1,)),
             dma((1,)),
+            dma((2,)),
+            dma((2,)),
+            dma((NG,)),
+            dma((NG,)),
             dma((2,)),
             dma((2,)),
         ],

time: 103 us -> 101 us (0.981)
  Pallas kernels: 100 us -> 97.1 us
    pallas_call x1, Pallas kernels: 100 us -> 97.1 us  [shards(): pl.pallas_call(kernel, out_shape=(out, out), in_specs=[hbm] * 6, out_spec...]
where the time goes in v3:
time: 101 us; the launch traced here: 100 us
  Pallas kernels  97.1 us (96%)
  local copies, waits for them, and re-layouts  2.72 us (3%)
    pallas_call x1, Pallas kernels, shards(): pl.pallas_call(kernel, out_shape=(out, out), in_specs=[hbm] * 6, out_spec...  97.1 us
    unnamed x4, local copies, waits for them, and re-layouts  2.72 us

profile of v3, /device:TPU:22, one launch (start us, length us, event | category | flops | bytes accessed | tf_op | source)
XLA Modules:
  0.0 100.5 jit_solution(7943416809639051640)
XLA Ops:
  0.6 97.1 %shard_map.77 = (f32[512,256]{1,0:T(8,128)}, f32[512,256]{1,0:T(8,128)}) custom-call(bf16[8,64,256]{2,1,0:T(8,128)(2,1)} %bitcast.3, bf16[2048,256]{1,0:T(8,128)(2,1)} %inw_ref.1, f32[2,128,128]{2,1,0:T(8,128)} %rec_hbm.1, f32[2,128]{1,0:T(2,128)} %bitcast.4, f32[2,128]{1,0:T(2,128)} %bitcast.5, f32[512,256]{1,0:T(8,128)} %guess_ref.1), custom_call_target="tpu_custom_call" | custom-call | tf_op jit(solution)/shard_map/pallas_call | solution.py:527
  97.7 0.0 copy-start
  97.7 1.9 %copy.10 = f32[512,256]{1,0:T(8,128)} copy(f32[512,256]{1,0:T(8,128)} %get-tuple-element.4) | data formatting | bytes 1048576
  99.7 0.0 copy-done
  99.7 0.8 copy.11
Async XLA Ops:
  97.7 1.9 %copy-start = (f32[512,256]{1,0:T(8,128)S(1)}, f32[512,256]{1,0:T(8,128)}, u32[]{:S(2)}) copy-start(f32[512,256]{1,0:T(8,128)} %get-tuple-element.5) | copy-start | bytes 1572868

commit v4 on v3

--- a/solution.py
+++ b/solution.py
@@ -337,7 +337,7 @@
             leaving[unit] = apply_map(entry[unit], whole)
             state_copy(unit, y).start()
 
-    def finish(h, unit, last=False):
+    def begin(h, unit, last=False):
         @pl.when(my_y == NY - 1)
         def _():
             state_copy(unit, NY - 1).wait_recv()
@@ -372,15 +372,21 @@
                 start_copy(h).start()
                 path_copy(h).wait_send()
 
-        advance(h, state, slope, offset, cur, PAD)
+        return state
+
+    def advance_step(h, state, step, slope, offset, out, base):
+        linear = folded(dot(pair(state), wc[h]))
+        state = linear * slope[h, pl.ds(step, B, stride=L), :]
+        state = state + offset[h, pl.ds(step, B, stride=L), :]
+        out[h, pl.ds(base + step, B, stride=L), :] = state
+        return state
 
     def advance(h, state, slope, offset, out, base):
-        weight = wc[h]
         for step in range(L):
-            linear = folded(dot(pair(state), weight))
-            state = linear * slope[h, pl.ds(step, B, stride=L), :]
-            state = state + offset[h, pl.ds(step, B, stride=L), :]
-            out[h, pl.ds(base + step, B, stride=L), :] = state
+            state = advance_step(h, state, step, slope, offset, out, base)
+
+    def finish(h, unit, last=False):
+        advance(h, begin(h, unit, last), slope, offset, cur, PAD)
 
     def unit_step(u, carry):
         sweep = u // 8
@@ -391,7 +397,7 @@
         def _():
             gather_chunk(g)
 
-        for unit, closes, passes in ((0, 7, (7, 8, 8)), (1, 9, (9, 10, 11)), (2, 13, (13, 14, 15))):
+        for unit, closes, passes in ((0, 6, (6, 7, 8)), (1, 9, (9, 10, 11)), (2, 13, (13, 14, 15))):
 
             @pl.when(u == closes)
             def _():
@@ -480,9 +486,29 @@
     def _():
         follow(0)
 
-    finish(1, 3, last=True)
+    state = begin(1, 3, last=True)
+    half_way = L // 2
+    for step in range(half_way):
+        state = advance_step(1, state, step, slope, offset, cur, PAD)
+
+    @pl.when(tm < NX * NY - 1)
+    def _():
+        start_copy(1).wait_recv()
+        own, following = state, norigin[1]
+        for step in range(L):
+            following = advance_step(1, following, step, nslope, noffset, ahead, 0)
+            if half_way + step < L:
+                own = advance_step(1, own, half_way + step, slope, offset, cur, PAD)
+
+    @pl.when(tm == NX * NY - 1)
+    def _():
+        own = state
+        for step in range(half_way, L):
+            own = advance_step(1, own, step, slope, offset, cur, PAD)
+        ahead[1] = jnp.broadcast_to(cur[1, PAD + T - 1 : PAD + T, :], (T, U))
+
     out_copy(1).start()
-    follow(1)
+    next_copy(1).start()
 
     def drain(g, carry):
         for kind, to in ((0, ahead_z), (1, back_z), (2, partner)):
@@ -524,7 +550,7 @@
     anywhere = pl.BlockSpec(memory_space=pl.ANY)
     out = jax.ShapeDtypeStruct((T, 2 * U), F32)
     dma = pltpu.SemaphoreType.DMA
-    return pl.pallas_call(
+    results = pl.pallas_call(
         kernel,
         out_shape=(out, out),
         in_specs=[hbm] * 6,
@@ -586,6 +612,34 @@
         initial.reshape(2, U),
         guess,
     )
+    return pl.pallas_call(
+        emit,
+        out_shape=(out, out),
+        in_specs=[anywhere] * 2,
+        out_specs=(anywhere, anywhere),
+        scratch_shapes=[pltpu.VMEM((2, T, 2 * U), F32), dma((4,)), dma((4,))],
+    )(*results)
+
+
+def emit(a_ref, b_ref, out_a, out_b, held, in_sem, out_sem):
+    half = T // 2
+    parts = [(k, pl.ds(half * i, half)) for k in range(2) for i in range(2)]
+    pairs = ((a_ref, out_a), (b_ref, out_b))
+    ins = [
+        pltpu.make_async_copy(pairs[k][0].at[rows], held.at[k, rows], in_sem.at[n])
+        for n, (k, rows) in enumerate(parts)
+    ]
+    outs = [
+        pltpu.make_async_copy(held.at[k, rows], pairs[k][1].at[rows], out_sem.at[n])
+        for n, (k, rows) in enumerate(parts)
+    ]
+    for copy in ins:
+        copy.start()
+    for arriving, leaving in zip(ins, outs):
+        arriving.wait()
+        leaving.start()
+    for copy in outs:
+        copy.wait()
 
 
 def solution(mesh):

time: 101 us -> 100 us (0.990)
  local copies, waits for them, and re-layouts: 2.72 us -> 0 us
  Pallas kernels: 97.1 us -> 99.3 us
    unnamed x4 -> x0, local copies, waits for them, and re-layouts: 2.72 us -> none
    pallas_call x0 -> x1, Pallas kernels: none -> 1.98 us  [shards(): pl.pallas_call(emit, out_shape=(out, out), in_specs=[anywhere] * 2, out_s...]
where the time goes in v4:
time: 100 us; the launch traced here: 99.9 us
  Pallas kernels  99.3 us (99%)
    pallas_call x1, Pallas kernels, shards(): pl.pallas_call(kernel, out_shape=(out, out), in_specs=[hbm] * 6, out_spec...  97.3 us

profile of v4, /device:TPU:22, one launch (start us, length us, event | category | flops | bytes accessed | tf_op | source)
XLA Modules:
  0.0 99.9 jit_solution(16188325193263805537)
XLA Ops:
  0.6 97.3 %shard_map.77 = (f32[512,256]{1,0:T(8,128)}, f32[512,256]{1,0:T(8,128)}) custom-call(bf16[8,64,256]{2,1,0:T(8,128)(2,1)} %bitcast.3, bf16[2048,256]{1,0:T(8,128)(2,1)} %inw_ref.1, f32[2,128,128]{2,1,0:T(8,128)} %rec_hbm.1, f32[2,128]{1,0:T(2,128)} %bitcast.4, f32[2,128]{1,0:T(2,128)} %bitcast.5, f32[512,256]{1,0:T(8,128)} %guess_ref.1), custom_call_target="tpu_custom_call" | custom-call | tf_op jit(solution)/shard_map/pallas_call | solution.py:553
  98.0 2.0 %shard_map.78 = (f32[512,256]{1,0:T(8,128)}, f32[512,256]{1,0:T(8,128)}) custom-call(f32[512,256]{1,0:T(8,128)} %get-tuple-element.4.a_ref, f32[512,256]{1,0:T(8,128)} %get-tuple-element.5.b_ref), custom_call_target="tpu_custom_call" | custom-call | tf_op jit(solution)/shard_map/pallas_call | solution.py:615

commit v5 on v4

--- a/solution.py
+++ b/solution.py
@@ -278,13 +278,18 @@
         weight = wc[h]
         vector = jnp.where(g == 0, 0.0, vec[h])
         for step in range(L):
-            for b in range(NB):
-                row = slope[h, pl.ds(first + (b * S + step), 1), :]
-                block = leaf.at[h, g, b] if step == 0 else work.at[b]
-                product = folded(dot(block[0:U, :], weight)) * row
-                out = leaf.at[h, g + 1, b] if step == L - 1 else work.at[b]
-                store_pair(out, pl.ds(0, U), product)
-            wide = folded(dot(pair(twice(vector)), weight))[0:NB]
+            for lead in range(0, NB, 2):
+                both = (lead, lead + 1)
+                blocks = [leaf.at[h, g, b] if step == 0 else work.at[b] for b in both]
+                left = [block[0:U, :] for block in blocks]
+                if lead == NB - 2:
+                    left.append(pair(twice(vector)))
+                product = folded(dot(jnp.concatenate(left, axis=0), weight))
+                for k, b in enumerate(both):
+                    row = slope[h, pl.ds(first + (b * S + step), 1), :]
+                    out = leaf.at[h, g + 1, b] if step == L - 1 else work.at[b]
+                    store_pair(out, pl.ds(0, U), product[k * U : (k + 1) * U] * row)
+            wide = product[2 * U : 2 * U + NB]
             vector = wide * slope[h, pl.ds(first + step, NB, stride=S), :]
             vector = vector + offset[h, pl.ds(first + step, NB, stride=S), :]
         vec[h] = vector

time: 100 us -> 96.9 us (0.969)
  Pallas kernels: 99.3 us -> 96.1 us
    pallas_call x1, Pallas kernels: 97.3 us -> 94.1 us  [shards(): pl.pallas_call(kernel, out_shape=(out, out), in_specs=[hbm] * 6, out_spec...]
where the time goes in v5:
time: 96.9 us; the launch traced here: 96.7 us
  Pallas kernels  96.1 us (99%)
    pallas_call x1, Pallas kernels, shards(): pl.pallas_call(kernel, out_shape=(out, out), in_specs=[hbm] * 6, out_spec...  94.1 us
    pallas_call x1, Pallas kernels, shards(): pl.pallas_call(emit, out_shape=(out, out), in_specs=[anywhere] * 2, out_s...  1.98 us

profile of v5, /device:TPU:22, one launch (start us, length us, event | category | flops | bytes accessed | tf_op | source)
XLA Modules:
  0.0 96.7 jit_solution(5391122661830512237)
XLA Ops:
  0.6 94.1 %shard_map.77 = (f32[512,256]{1,0:T(8,128)}, f32[512,256]{1,0:T(8,128)}) custom-call(bf16[8,64,256]{2,1,0:T(8,128)(2,1)} %bitcast.3, bf16[2048,256]{1,0:T(8,128)(2,1)} %inw_ref.1, f32[2,128,128]{2,1,0:T(8,128)} %rec_hbm.1, f32[2,128]{1,0:T(2,128)} %bitcast.4, f32[2,128]{1,0:T(2,128)} %bitcast.5, f32[512,256]{1,0:T(8,128)} %guess_ref.1), custom_call_target="tpu_custom_call" | custom-call | tf_op jit(solution)/shard_map/pallas_call | solution.py:558
  94.8 2.0 %shard_map.78 = (f32[512,256]{1,0:T(8,128)}, f32[512,256]{1,0:T(8,128)}) custom-call(f32[512,256]{1,0:T(8,128)} %get-tuple-element.4.a_ref, f32[512,256]{1,0:T(8,128)} %get-tuple-element.5.b_ref), custom_call_target="tpu_custom_call" | custom-call | tf_op jit(solution)/shard_map/pallas_call | solution.py:620

commit v6 on v5

--- a/solution.py
+++ b/solution.py
@@ -278,18 +278,18 @@
         weight = wc[h]
         vector = jnp.where(g == 0, 0.0, vec[h])
         for step in range(L):
-            for lead in range(0, NB, 2):
-                both = (lead, lead + 1)
+            for lead in range(0, NB, 4):
+                both = range(lead, lead + 4)
                 blocks = [leaf.at[h, g, b] if step == 0 else work.at[b] for b in both]
                 left = [block[0:U, :] for block in blocks]
-                if lead == NB - 2:
+                if lead == NB - 4:
                     left.append(pair(twice(vector)))
                 product = folded(dot(jnp.concatenate(left, axis=0), weight))
                 for k, b in enumerate(both):
                     row = slope[h, pl.ds(first + (b * S + step), 1), :]
                     out = leaf.at[h, g + 1, b] if step == L - 1 else work.at[b]
                     store_pair(out, pl.ds(0, U), product[k * U : (k + 1) * U] * row)
-            wide = product[2 * U : 2 * U + NB]
+            wide = product[4 * U : 4 * U + NB]
             vector = wide * slope[h, pl.ds(first + step, NB, stride=S), :]
             vector = vector + offset[h, pl.ds(first + step, NB, stride=S), :]
         vec[h] = vector

time: 96.9 us -> 97.3 us (level)
  no operation moved by 1% of the time
where the time goes in v6:
time: 97.3 us; the launch traced here: 97.2 us
  Pallas kernels  96.5 us (99%)
    pallas_call x1, Pallas kernels, shards(): pl.pallas_call(kernel, out_shape=(out, out), in_specs=[hbm] * 6, out_spec...  94.6 us
    pallas_call x1, Pallas kernels, shards(): pl.pallas_call(emit, out_shape=(out, out), in_specs=[anywhere] * 2, out_s...  1.98 us

profile of v6, /device:TPU:22, one launch (start us, length us, event | category | flops | bytes accessed | tf_op | source)
XLA Modules:
  0.0 97.2 jit_solution(9582863131229488769)
XLA Ops:
  0.6 94.6 %shard_map.77 = (f32[512,256]{1,0:T(8,128)}, f32[512,256]{1,0:T(8,128)}) custom-call(bf16[8,64,256]{2,1,0:T(8,128)(2,1)} %bitcast.3, bf16[2048,256]{1,0:T(8,128)(2,1)} %inw_ref.1, f32[2,128,128]{2,1,0:T(8,128)} %rec_hbm.1, f32[2,128]{1,0:T(2,128)} %bitcast.4, f32[2,128]{1,0:T(2,128)} %bitcast.5, f32[512,256]{1,0:T(8,128)} %guess_ref.1), custom_call_target="tpu_custom_call" | custom-call | tf_op jit(solution)/shard_map/pallas_call | solution.py:558
  95.2 2.0 %shard_map.78 = (f32[512,256]{1,0:T(8,128)}, f32[512,256]{1,0:T(8,128)}) custom-call(f32[512,256]{1,0:T(8,128)} %get-tuple-element.4.a_ref, f32[512,256]{1,0:T(8,128)} %get-tuple-element.5.b_ref), custom_call_target="tpu_custom_call" | custom-call | tf_op jit(solution)/shard_map/pallas_call | solution.py:620
